TPU v7x, 32 devices: a whole 2x2x4 slice. The times are simulated.
32 devices in a mesh: dp: 4 (over z), ctx: 8 (over y, x, core).
Axes of the slice: x: 2, y: 2, z: 4, core: 2. Of those that a mesh axis runs over, the one named last changes fastest.
Arguments:
- inputs: bfloat16 [4, 1024, 1024], P('dp', 'ctx'), may hold values from -6 to 6
- cotangent: bfloat16 [4, 1024, 1024], P('dp', 'ctx'), may hold values from -6 to 6
- mixer_params: float32 [4194304], P(('dp', 'ctx')), may hold values from -0.1875 to 0.1875
- mixer_first: float32 [4194304], P(('dp', 'ctx')), may hold values from -0.0014648438 to 0.0014648438
- mixer_second: float32 [4194304], P(('dp', 'ctx')), may hold values from 2.3434208e-11 to 2.3434207e-10
- ffn_params: float32 [4325376], P(('dp', 'ctx')), may hold values from -0.21320072 to 0.21320072
- ffn_first: float32 [4325376], P(('dp', 'ctx')), may hold values from -0.0014648438 to 0.0014648438
- ffn_second: float32 [4325376], P(('dp', 'ctx')), may hold values from 2.3434208e-11 to 2.3434207e-10
- small_params: float32 [14852], replicated, may hold values from -7 to 2.8
- small_first: float32 [14852], replicated, may hold values from -0.0014648438 to 0.0014648438
- small_second: float32 [14852], replicated, may hold values from 2.3434208e-11 to 2.3434208e-07
Outputs:
- outputs: bfloat16 [4, 1024, 1024], P('dp', 'ctx')
- grad_inputs: bfloat16 [4, 1024, 1024], P('dp', 'ctx')
- mixer_grad: float32 [4194304], P(('dp', 'ctx'))
- ffn_grad: float32 [4325376], P(('dp', 'ctx'))
- small_grad: float32 [14852], replicated
- mixer_new: float32 [4194304], P(('dp', 'ctx'))
- mixer_first_new: float32 [4194304], P(('dp', 'ctx'))
- mixer_second_new: float32 [4194304], P(('dp', 'ctx'))
- ffn_new: float32 [4325376], P(('dp', 'ctx'))
- ffn_first_new: float32 [4325376], P(('dp', 'ctx'))
- ffn_second_new: float32 [4325376], P(('dp', 'ctx'))
- small_new: float32 [14852], replicated
- small_first_new: float32 [14852], replicated
- small_second_new: float32 [14852], replicated
All inputs are finite; a program needn't handle non-finite values.
Results may differ from a plain program's by a relative error of at most 0.013.
Values may be sent and summed in bfloat16 or wider, within the bound.
A program may use at most 320 MiB of HBM per device.

v0:
```python
import jax
import jax.numpy as jnp
from jax import lax
from jax.sharding import PartitionSpec as P

D = 1024
H = 2
DK = 256
DV = 512
FF = 1408
CONV = 4
GROUP = 64
EPSILON = 1e-06
ADAM_EPS = 1e-08
LEARN_RATE = 0.02
BETA_ONE = 0.9
BETA_TWO = 0.999
DECAY_RATE = 0.1
CORRECT_ONE = 1.0 - 0.9**3
CORRECT_TWO = 1.0 - 0.999**3
MAX_NORM = 1.0
HIGHEST = lax.Precision.HIGHEST


def from_behind(value, axis, steps):
    count = lax.axis_size(axis)
    initial, last = (max(0, -steps), min(count, count - steps))
    return lax.ppermute(value, axis, [(source, source + steps) for source in range(initial, last)])


def entering(array, axis, combine, identity):
    devices, position = (lax.axis_size(axis), lax.axis_index(axis))
    everything = jax.tree.map(
        lambda part, kind: lax.all_gather(part.astype(kind), axis),
        array,
        (jnp.bfloat16, jnp.bfloat16),
    )
    start = jax.tree.map(
        lambda part, zero: jnp.broadcast_to(jnp.asarray(zero, part.dtype), part.shape),
        array,
        identity,
    )

    def lap(k, before):
        reached = k < position
        new = combine(
            before, jax.tree.map(lambda part, own: part[k].astype(own.dtype), everything, array)
        )
        return jax.tree.map(lambda a, b: jnp.where(reached, a, b), new, before)

    return lax.fori_loop(0, devices, lap, start)


def carried_in(array, axis, join, neutral):
    count = lax.axis_size(axis)
    place = lax.axis_index(axis)
    ahead = count - 1 - place
    gathered = jax.tree.map(
        lambda a, kind: lax.all_gather(a.astype(kind), axis),
        array,
        jax.tree.map(lambda a: jnp.bfloat16 if a.dtype == jnp.float32 else a.dtype, array),
    )
    state = jax.tree.map(lambda a, e: jnp.zeros_like(a) + jnp.asarray(e, a.dtype), array, neutral)

    def one(lap, state):
        source = count - 1 - lap
        return join(
            state,
            jax.tree.map(
                lambda a, own: lax.dynamic_index_in_dim(a, source, 0, False).astype(own.dtype),
                gathered,
                array,
            ),
        )

    return lax.fori_loop(0, ahead, one, state)


def norm_scale(values, gain):
    return values * lax.rsqrt(jnp.mean(values * values, axis=-1, keepdims=True) + EPSILON) * gain


def swiglu(gate_part, up_part):
    return jax.nn.silu(gate_part) * up_part


def unpack_small(packed):
    width = 2 * H * DK + H * DV
    lengths = [D, D, DV, CONV * width, D * 2 * H, H, H]
    pieces = []
    offset = 0
    for length in lengths:
        pieces.append(packed[offset : offset + length])
        offset = offset + length
    return (
        pieces[0],
        pieces[1],
        pieces[2],
        pieces[3].reshape(CONV, width),
        pieces[4].reshape(D, 2 * H),
        pieces[5],
        pieces[6],
    )


def split_weights(mix_whole, ffn_whole):
    mix_rows = mix_whole.reshape(-1, D)
    ffn_rows = ffn_whole.reshape(-1, D)
    edge = 2 * H * DK + 2 * H * DV
    return (mix_rows[:edge], mix_rows[edge:], ffn_rows[: 2 * FF], ffn_rows[2 * FF :])


def features(extended, tap_values, gate_logits, a_log, dt_bias):
    count = extended.shape[0] - (CONV - 1)
    summed = tap_values[0] * extended[0:count]
    for tap_index in range(1, CONV):
        summed = summed + tap_values[tap_index] * extended[tap_index : tap_index + count]
    activated = jax.nn.silu(summed)
    query_part = activated[:, : H * DK].reshape(count, H, DK)
    key_part = activated[:, H * DK : 2 * H * DK].reshape(count, H, DK)
    value_part = activated[:, 2 * H * DK :].reshape(count, H, DV)
    query = (
        query_part
        * lax.rsqrt(jnp.sum(query_part * query_part, axis=-1, keepdims=True) + EPSILON)
        * DK ** (-0.5)
    )
    keys = key_part * lax.rsqrt(jnp.sum(key_part * key_part, axis=-1, keepdims=True) + EPSILON)
    beta = jax.nn.sigmoid(gate_logits[:, :H])
    decay = -jnp.exp(a_log) * jax.nn.softplus(gate_logits[:, H:] + dt_bias)
    return (
        jnp.transpose(query, (1, 0, 2)),
        jnp.transpose(keys, (1, 0, 2)),
        jnp.transpose(value_part, (1, 0, 2)),
        beta.T,
        decay.T,
    )


def split_groups(values):
    blocks = values.shape[1] // GROUP
    shaped = values.reshape((values.shape[0], blocks, GROUP) + values.shape[2:])
    return jnp.moveaxis(shaped, 1, 0)


def group_parts(key_block, value_block, beta_block, decay_block):
    size = decay_block.shape[-1]
    cumulative = jnp.cumsum(decay_block, axis=-1)
    row_index = lax.broadcasted_iota(jnp.int32, (size, size), 0)
    col_index = lax.broadcasted_iota(jnp.int32, (size, size), 1)
    lower = row_index >= col_index
    strict = row_index > col_index
    spread = jnp.where(lower, cumulative[:, :, None] - cumulative[:, None, :], 0.0)
    decay_matrix = jnp.where(lower, jnp.exp(spread), 0.0)
    key_gram = jnp.einsum("hid,hjd->hij", key_block, key_block, precision=HIGHEST)
    system = jnp.where(strict, beta_block[:, :, None] * key_gram * decay_matrix, 0.0) + jnp.eye(
        size, dtype=key_block.dtype
    )
    right_side = jnp.concatenate(
        [
            key_block * (beta_block * jnp.exp(cumulative))[:, :, None],
            value_block * beta_block[:, :, None],
        ],
        axis=-1,
    )
    solved = jax.scipy.linalg.solve_triangular(system, right_side, lower=True, unit_diagonal=True)
    key_mix = solved[..., :DK]
    value_mix = solved[..., DK:]
    last_decay = cumulative[:, -1]
    keys_to_end = key_block * jnp.exp(last_decay[:, None] - cumulative)[:, :, None]
    return (cumulative, decay_matrix, key_mix, value_mix, last_decay, keys_to_end)


def group_run(state, pieces):
    query_block, key_block, value_block, beta_block, decay_block = pieces
    cumulative, decay_matrix, key_mix, value_mix, last_decay, keys_to_end = group_parts(
        key_block, value_block, beta_block, decay_block
    )
    pseudo_values = value_mix - jnp.einsum("hcd,hde->hce", key_mix, state, precision=HIGHEST)
    scores = jnp.einsum("hid,hjd->hij", query_block, key_block, precision=HIGHEST) * decay_matrix
    block_out = jnp.einsum(
        "hcd,hde->hce", query_block * jnp.exp(cumulative)[:, :, None], state, precision=HIGHEST
    )
    block_out = block_out + jnp.einsum("hij,hje->hie", scores, pseudo_values, precision=HIGHEST)
    next_state = jnp.exp(last_decay)[:, None, None] * state + jnp.einsum(
        "hcd,hce->hde", keys_to_end, pseudo_values, precision=HIGHEST
    )
    return (next_state, block_out)


def mixer_run(state, query, keys, values, beta, decay):
    pieces = (
        split_groups(query),
        split_groups(keys),
        split_groups(values),
        split_groups(beta),
        split_groups(decay),
    )
    final_state, blocks_out = lax.scan(group_run, state, pieces)
    joined = jnp.moveaxis(blocks_out, 0, 1)
    return (joined.reshape(joined.shape[0], -1, joined.shape[-1]), final_state)


def combine(earlier, later):
    first_map, first_shift = earlier
    second_map, second_shift = later
    composed = jnp.einsum("hij,hjk->hik", second_map, first_map, precision=HIGHEST)
    shifted = jnp.einsum("hij,hjk->hik", second_map, first_shift, precision=HIGHEST) + second_shift
    return (composed, shifted)


def transition(keys, values, beta, decay):
    pieces = (split_groups(keys), split_groups(values), split_groups(beta), split_groups(decay))
    start = (
        jnp.broadcast_to(jnp.eye(DK, dtype=jnp.float32), (H, DK, DK)),
        jnp.zeros((H, DK, DV), jnp.float32),
    )

    def step_block(carry, piece):
        key_block, value_block, beta_block, decay_block = piece
        cumulative, decay_matrix, key_mix, value_mix, last_decay, keys_to_end = group_parts(
            key_block, value_block, beta_block, decay_block
        )
        block_map = jnp.exp(last_decay)[:, None, None] * jnp.eye(
            DK, dtype=key_block.dtype
        ) - jnp.einsum("hcd,hce->hde", keys_to_end, key_mix, precision=HIGHEST)
        block_shift = jnp.einsum("hcd,hce->hde", keys_to_end, value_mix, precision=HIGHEST)
        return (combine(carry, (block_map, block_shift)), None)

    result, unused = lax.scan(step_block, start, pieces)
    return result


def gated_norm(mixed, out_gate, gain_head):
    count = out_gate.shape[0]
    heads = jnp.transpose(mixed, (1, 0, 2))
    normed = norm_scale(heads, gain_head)
    return (normed * jax.nn.silu(out_gate.reshape(count, H, DV))).reshape(count, H * DV)


def adam_step(weight, grad_full, first, second, clip):
    grad_clipped = grad_full * clip
    first_new = BETA_ONE * first + (1.0 - BETA_ONE) * grad_clipped
    second_new = BETA_TWO * second + (1.0 - BETA_TWO) * grad_clipped * grad_clipped
    update = (
        first_new / CORRECT_ONE / (jnp.sqrt(second_new / CORRECT_TWO) + ADAM_EPS)
        + DECAY_RATE * weight
    )
    return (weight - LEARN_RATE * update, first_new, second_new)


def body(
    inputs,
    cotangent,
    mixer_params,
    mixer_first,
    mixer_second,
    ffn_params,
    ffn_first,
    ffn_second,
    small_params,
    small_first,
    small_second,
):
    gain_one, gain_two, gain_head, tap_values, w_gates, a_log, dt_bias = unpack_small(small_params)
    width = tap_values.shape[1]
    mix_part = mixer_params.astype(jnp.bfloat16)
    ffn_part = ffn_params.astype(jnp.bfloat16)
    mix_whole, ffn_whole = (
        lax.all_gather(mix_part, ("dp", "ctx"), axis=0, tiled=True),
        lax.all_gather(ffn_part, ("dp", "ctx"), axis=0, tiled=True),
    )
    w_in, w_out, w_ffn, w_down = split_weights(mix_whole, ffn_whole)
    x_float = inputs[0].astype(jnp.float32)
    count = x_float.shape[0]
    normed_in = norm_scale(x_float, gain_one).astype(jnp.bfloat16)
    projected = jnp.dot(normed_in, w_in.T, preferred_element_type=jnp.float32)
    gate_logits = jnp.dot(normed_in.astype(jnp.float32), w_gates, precision=HIGHEST)
    conv_pre = projected[:, :width]
    out_gate = projected[:, width:]
    border = from_behind(conv_pre[count - (CONV - 1) :], "ctx", 1)
    extended = jnp.concatenate([border, conv_pre], axis=0)
    query, keys, values, beta, decay = features(extended, tap_values, gate_logits, a_log, dt_bias)
    maps = transition(keys, values, beta, decay)
    eye_stack = jnp.broadcast_to(jnp.eye(DK, dtype=jnp.float32), (H, DK, DK))
    zero_stack = jnp.zeros((H, DK, DV), jnp.float32)
    prefix = entering((maps[0], maps[1]), "ctx", combine, (eye_stack, zero_stack))
    state_in = prefix[1]
    mixed, final_state = mixer_run(state_in, query, keys, values, beta, decay)
    head_out = gated_norm(mixed, out_gate, gain_head).astype(jnp.bfloat16)
    resid = x_float + jnp.dot(head_out, w_out, preferred_element_type=jnp.float32)
    normed_mid = norm_scale(resid, gain_two).astype(jnp.bfloat16)
    ffn_pre = jnp.dot(normed_mid, w_ffn.T, preferred_element_type=jnp.float32)
    gate_part = ffn_pre[:, :FF]
    up_part = ffn_pre[:, FF:]
    hidden_act = swiglu(gate_part, up_part).astype(jnp.bfloat16)
    result = (resid + jnp.dot(hidden_act, w_down, preferred_element_type=jnp.float32)).astype(
        jnp.bfloat16
    )
    seq_grad = cotangent[0]
    grad_float = seq_grad.astype(jnp.float32)
    grad_down = jnp.dot(hidden_act.T, seq_grad, preferred_element_type=jnp.float32)
    grad_hidden = jnp.dot(seq_grad, w_down.T, preferred_element_type=jnp.float32)
    unused_one, pull_swiglu = jax.vjp(swiglu, gate_part, up_part)
    grad_gate, grad_up = pull_swiglu(grad_hidden)
    grad_pre = jnp.concatenate([grad_gate, grad_up], axis=1).astype(jnp.bfloat16)
    grad_ffn = jnp.dot(grad_pre.T, normed_mid, preferred_element_type=jnp.float32)
    grad_mid = jnp.dot(grad_pre, w_ffn, preferred_element_type=jnp.float32)
    unused_two, pull_mid = jax.vjp(norm_scale, resid, gain_two)
    grad_through, grad_gain_two = pull_mid(grad_mid)
    grad_resid = grad_float + grad_through
    ffn_flat = jnp.concatenate([grad_ffn, grad_down], axis=0).reshape(-1)
    ffn_shard = lax.psum_scatter(ffn_flat, ("dp", "ctx"), scatter_dimension=0, tiled=True)
    resid_half = grad_resid.astype(jnp.bfloat16)
    grad_out = jnp.dot(head_out.T, resid_half, preferred_element_type=jnp.float32)
    grad_head = jnp.dot(resid_half, w_out.T, preferred_element_type=jnp.float32)
    unused_three, pull_gated = jax.vjp(gated_norm, mixed, out_gate, gain_head)
    grad_mixed, grad_gate_out, grad_gain_head = pull_gated(grad_head)
    unused_four, pull_mixer = jax.vjp(mixer_run, state_in, query, keys, values, beta, decay)
    local_term = pull_mixer((grad_mixed, jnp.zeros_like(final_state)))[0]
    flipped = jnp.transpose(maps[0], (0, 2, 1))
    suffix = carried_in((flipped, local_term), "ctx", combine, (eye_stack, zero_stack))
    mixer_grads = pull_mixer((grad_mixed, suffix[1]))
    unused_five, pull_feat = jax.vjp(features, extended, tap_values, gate_logits, a_log, dt_bias)
    grad_ext, grad_taps, grad_logits, grad_alog, grad_bias = pull_feat(mixer_grads[1:])
    returned = from_behind(grad_ext[: CONV - 1], "ctx", -1)
    grad_conv = grad_ext[CONV - 1 :].at[count - (CONV - 1) :].add(returned)
    grad_proj = jnp.concatenate([grad_conv, grad_gate_out], axis=1).astype(jnp.bfloat16)
    grad_in = jnp.dot(grad_proj.T, normed_in, preferred_element_type=jnp.float32)
    grad_normed = jnp.dot(grad_proj, w_in, preferred_element_type=jnp.float32) + jnp.dot(
        grad_logits, w_gates.T, precision=HIGHEST
    )
    grad_gates = jnp.dot(normed_in.astype(jnp.float32).T, grad_logits, precision=HIGHEST)
    unused_six, pull_in = jax.vjp(norm_scale, x_float, gain_one)
    grad_x, grad_gain_one = pull_in(grad_normed)
    grad_input = (grad_resid + grad_x).astype(jnp.bfloat16)
    mix_flat = jnp.concatenate([grad_in, grad_out], axis=0).reshape(-1)
    mix_shard = lax.psum_scatter(mix_flat, ("dp", "ctx"), scatter_dimension=0, tiled=True)
    small_local = jnp.concatenate(
        [
            grad_gain_one,
            grad_gain_two,
            grad_gain_head,
            grad_taps.reshape(-1),
            grad_gates.reshape(-1),
            grad_alog,
            grad_bias,
        ]
    )
    shard_squares = jnp.sum(mix_shard * mix_shard) + jnp.sum(ffn_shard * ffn_shard)
    small_grad, total_squares = lax.psum((small_local, shard_squares), ("dp", "ctx"))
    squares = total_squares + jnp.sum(small_grad * small_grad)
    clip = jnp.minimum(1.0, MAX_NORM / (jnp.sqrt(squares) + 1e-06))
    mixer_new, mixer_first_new, mixer_second_new = adam_step(
        mixer_params, mix_shard, mixer_first, mixer_second, clip
    )
    ffn_new, ffn_first_new, ffn_second_new = adam_step(
        ffn_params, ffn_shard, ffn_first, ffn_second, clip
    )
    small_new, small_first_new, small_second_new = adam_step(
        small_params, small_grad, small_first, small_second, clip
    )
    return (
        result[None],
        grad_input[None],
        mix_shard,
        ffn_shard,
        small_grad,
        mixer_new,
        mixer_first_new,
        mixer_second_new,
        ffn_new,
        ffn_first_new,
        ffn_second_new,
        small_new,
        small_first_new,
        small_second_new,
    )


def solution(mesh):
    return jax.shard_map(
        body,
        mesh=mesh,
        in_specs=(
            P("dp", "ctx", None),
            P("dp", "ctx", None),
            P(("dp", "ctx")),
            P(("dp", "ctx")),
            P(("dp", "ctx")),
            P(("dp", "ctx")),
            P(("dp", "ctx")),
            P(("dp", "ctx")),
            P(),
            P(),
            P(),
        ),
        out_specs=(
            P("dp", "ctx", None),
            P("dp", "ctx", None),
            P(("dp", "ctx")),
            P(("dp", "ctx")),
            P(),
            P(("dp", "ctx")),
            P(("dp", "ctx")),
            P(("dp", "ctx")),
            P(("dp", "ctx")),
            P(("dp", "ctx")),
            P(("dp", "ctx")),
            P(),
            P(),
            P(),
        ),
        check_vma=False,
    )
```

profile of v0, /device:TPU:0, one launch (start us, length us, event | category | flops | bytes accessed | tf_op | source)
XLA Modules:
  0.0 1128.1 jit_solution(17236866343093623935)
XLA Ops:
  13.7 77.5 %all-gather.11.cloned.1.call-done = bf16[4194304]{0:T(1024)(128)(2,1)} async-done(((bf16[131072]{0:T(1024)(128)(2,1)}), bf16[4194304]{0:T(1024)(128)(2,1)}) %all-gather.11.cloned.1.call-update) | async-done | bytes 8388624 | tf_op jit(solution)/shard_map/all_gather | solution.py:269
  91.2 6.4 slice.294
  97.7 10.3 slice.251
  108.0 5.0 fusion.320
  121.7 38.8 %while.160 = (s32[]{:T(128)}, f32[2,256,256]{2,1,0:T(8,128)}, f32[2,256,512]{2,1,0:T(8,128)}, f32[2,2,64]{2,1,0:T(2,128)}, f32[2,2,64,256]{3,2,1,0:T(8,128)S(1)}...) while((s32[]{:T(128)}, f32[2,256,256]{2,1,0:T(8,128)}, ...), condition=%wide.region_4.6_spmd.clone, body=%wide.region_2.5_spmd.clone.sunk | while | flops 1611903232 | bytes 17252060 | solution.py:229
  124.1 9.8 custom-call.53
  143.5 9.8 custom-call.53
  175.4 4.2 slice.275
  183.7 6.1 slice.306
  189.8 9.7 slice.270
  202.5 5.5 slice.274
  208.1 31.5 %all-gather.17.cloned.1.call-done = bf16[16,256,512]{2,1,0:T(8,128)(2,1)} async-done(((bf16[2,256,512]{2,1,0:T(8,128)(2,1)}), bf16[16,256,512]{2,1,0:T(8,128)(2,1)}) %all-gather.17.cloned.1.call-update) | async-done | bytes 4194320 | tf_op jit(solution)/shard_map/all_gather | solution.py:34
  239.6 16.6 %while.161 = (s32[]{:T(128)}, f32[2,256,512]{2,1,0:T(8,128)S(1)}, s32[]{:T(128)}, bf16[8,2,256,256]{3,2,1,0:T(8,128)(2,1)}, bf16[8,2,256,512]{3,2,1,0:T(8,128)(2,1)}, /*index=5*/s32[]{:T(128)}, s32[]{:T(128)}) while((s32[]{:T(128)}, f32[2,256,512]{2,1,0:T(8,128)S(1)}, s32[]{:T(128)}, bf16[8,2,256,256]{3,2,1,0:T(8,128)(2,1)}, ...), condition=%wide.region_6.8_spmd.clone, body=%wide.region_5.7_spmd.clone.sunk | while | flops 806617088 | bytes 6031975 | solution.py:51
  257.2 52.2 %while.156 = (s32[]{:T(128)}, f32[2,256,512]{2,1,0:T(8,128)S(1)}, f32[2,2,64,512]{3,2,1,0:T(8,128)}, f32[2,2,64]{2,1,0:T(2,128)}, f32[2,2,64,256]{3,2,1,0:T(8,12...) while((s32[]{:T(128)}, f32[2,256,512]{2,1,0:T(8,128)S(1)}, ...), condition=%wide.region_10.12_spmd, body=%wide.region_8.11_spmd.sunk | while | flops 781201600 | bytes 15008757 | solution.py:198
  266.8 11.2 custom-call.50
  292.9 11.2 custom-call.50
  321.2 69.0 %while.158 = (s32[]{:T(128)}, f32[2,256,512]{2,1,0:T(8,128)S(1)}, f32[2,2,64,64]{3,2,1,0:T(8,128)}, f32[2,2,64,64]{3,2,1,0:T(8,128)}, f32[2,2,64,1]{2,1,3,0:T(2,...) while((s32[]{:T(128)}, f32[2,256,512]{2,1,0:T(8,128)S(1)}, ...), condition=%wide.region_17.19_spmd.clone.clone, body=%wide.region_15.18_spmd.clone.clone.sunk | while | flops 529560128 | bytes 10886193 | solution.py:198
  330.0 11.2 custom-call.51
  359.6 11.2 custom-call.51
  390.2 5.0 fusion.317
  402.4 15.0 %while.162 = (s32[]{:T(128)}, f32[2,256,512]{2,1,0:T(8,128)S(1)}, f32[2,2,1,1]{1,3,2,0:T(1,128)}, f32[2,2,64,256]{3,2,1,0:T(8,128)}, f32[2,2,64,512]{3,2,1,0:T(8...) while((s32[]{:T(128)}, f32[2,256,512]{2,1,0:T(8,128)S(1)}, ...), condition=%wide.region_19.21_spmd.clone, body=%wide.region_18.20_spmd.clone.sunk | while | flops 655753216 | bytes 7277727 | solution.py:198
  425.4 5.7 maximum_bitcast_fusion
  431.1 8.3 copy.331
  442.2 12.9 %all-gather.21.cloned.1.call-done = bf16[16,256,512]{2,1,0:T(8,128)(2,1)} async-done(((bf16[2,256,512]{2,1,0:T(8,128)(2,1)}), bf16[16,256,512]{2,1,0:T(8,128)(2,1)}) %all-gather.21.cloned.1.call-update) | async-done | bytes 4194320 | tf_op jit(solution)/shard_map/all_gather | solution.py:59
  455.3 13.4 %while.157 = (s32[]{:T(128)}, f32[2,256,512]{2,1,0:T(8,128)S(1)}, s32[]{:T(128)}, bf16[8,2,256,256]{3,2,1,0:T(8,128)(2,1)}, bf16[8,2,256,512]{3,2,1,0:T(8,128)(2...) while((s32[]{:T(128)}, f32[2,256,512]{2,1,0:T(8,128)S(1)}, s32[]{:T(128)}, ...), condition=%wide.region_21.23_spmd, body=%wide.region_20.22_spmd.sunk | while | flops 805830656 | bytes 4981907 | solution.py:76
  472.2 67.0 %while.159 = (s32[]{:T(128)}, f32[2,256,512]{2,1,0:T(8,128)S(1)}, f32[2,2,64,256]{3,2,0,1:T(8,128)}, f32[2,2,64,256]{3,2,0,1:T(8,128)}, f32[2,2,64,512]{3,2,0,1:...) while((s32[]{:T(128)}, f32[2,256,512]{2,1,0:T(8,128)S(1)}, ...), condition=%wide.region_33.35_spmd.clone.clone, body=%wide.region_22.34_spmd.clone.clone.sunk | while | flops 1569133696 | bytes 51536812 | solution.py:198
  479.0 9.8 custom-call.52
  512.3 9.8 custom-call.52
  551.6 5.3 maximum_bitcast_fusion.1
  556.9 8.1 copy.330
  576.6 491.6 %all-reduce.22.cloned.1.call-done = (f32[4194304]{0:T(1024)}, f32[4325376]{0:T(1024)}) async-done(((f32[4194304]{0:T(1024)}, f32[4325376]{0:T(1024)}), (f32[4194304]{0:T(1024)}, f32[4325376]{0:T(1024)})) %all-reduce.22.cloned.1.call-update) | async-done | bytes 34078736
  1073.2 40.8 %all-reduce.18 = (f32[14852]{0:T(1024)S(1)}, f32[]{:T(128)}) all-reduce(f32[14852]{0:T(1024)S(1)} %concatenate.40, f32[]{:T(128)S(6)} %add.447), channel_id=1, replica_groups=mesh['dp'=4,'ctx'=8] {'dp','ctx'}, use_global_device_ids=true, to_apply=%region_48.50 | all-reduce | flops 14853 | bytes 118824 | tf_op jit(solution)/shard_map/psum | solution.py:350
  (747 shorter events, 279.1 us)
Async XLA Ops:
  7.2 84.0 %all-gather.11.cloned.1.call-start = ((), (), s32[]{:S(2)}) async-start(), calls=%async_computation | async-start | bytes 8650752 | tf_op jit(solution)/shard_map/all_gather | solution.py:269
  9.1 174.6 %all-gather.13.cloned.1.call-start = ((), (), s32[]{:S(2)}) async-start(), calls=%async_computation.1 | async-start | bytes 8921088 | tf_op jit(solution)/shard_map/all_gather | solution.py:270
  10.9 197.1 %all-gather.15.cloned.1.call-start = ((), (), s32[]{:S(2)}) async-start(), calls=%async_computation.2 | async-start | bytes 2359296 | tf_op jit(solution)/shard_map/all_gather | solution.py:34
  11.6 86.1 %copy-start.28 = (f32[1024,4]{1,0:T(8,128)}, f32[1024,4]{1,0:T(8,128)S(1)}, u32[]{:S(2)}) copy-start(f32[1024,4]{1,0:T(8,128)S(1)} %reshape.844) | copy-start | bytes 49156
  11.7 96.3 %copy-start.95 = (f32[128]{0:T(128)}, f32[128]{0:T(128)S(1)}, u32[]{:S(2)}) copy-start(f32[128]{0:T(128)S(1)} %fusion.309) | copy-start | bytes 1540
  11.8 85.9 %copy-start.121 = (f32[2]{0:T(128)}, f32[2]{0:T(128)S(1)}, u32[]{:S(2)}) copy-start(f32[2]{0:T(128)S(1)} %get-tuple-element.2850) | copy-start | bytes 28
  11.8 85.9 %copy-start.123 = (f32[2]{0:T(128)}, f32[2]{0:T(128)S(1)}, u32[]{:S(2)}) copy-start(f32[2]{0:T(128)S(1)} %get-tuple-element.2851) | copy-start | bytes 28
  12.4 95.6 %copy-start.69 = (f32[1024]{0:T(1024)}, f32[1024]{0:T(1024)S(1)}, u32[]{:S(2)}) copy-start(f32[1024]{0:T(1024)S(1)} %get-tuple-element.2845) | copy-start | bytes 12292
  13.0 84.7 %copy-start.98 = (f32[128,4]{0,1:T(4,128)}, f32[128,4]{0,1:T(4,128)S(1)}, u32[]{:S(2)}) copy-start(f32[128,4]{0,1:T(4,128)S(1)} %fusion.282) | copy-start | bytes 6148
  13.6 102.3 %copy-start.113 = (f32[128,2]{0,1:T(2,128)}, f32[128,2]{0,1:T(2,128)S(1)}, u32[]{:S(2)}) copy-start(f32[128,2]{0,1:T(2,128)S(1)} %get-tuple-element.2853) | copy-start | bytes 3076
  13.7 103.1 %copy-start.77 = (f32[2048]{0:T(1024)}, f32[2048]{0:T(1024)S(1)}, u32[]{:S(2)}) copy-start(f32[2048]{0:T(1024)S(1)} %get-tuple-element.2846) | copy-start | bytes 24580
  13.7 103.1 %copy-start.79 = (f32[2048]{0:T(1024)}, f32[2048]{0:T(1024)S(1)}, u32[]{:S(2)}) copy-start(f32[2048]{0:T(1024)S(1)} %get-tuple-element.2847) | copy-start | bytes 24580
  13.7 103.1 %copy-start.81 = (f32[2048]{0:T(1024)}, f32[2048]{0:T(1024)S(1)}, u32[]{:S(2)}) copy-start(f32[2048]{0:T(1024)S(1)} %get-tuple-element.2848) | copy-start | bytes 24580
  13.7 103.1 %copy-start.83 = (f32[2048]{0:T(1024)}, f32[2048]{0:T(1024)S(1)}, u32[]{:S(2)}) copy-start(f32[2048]{0:T(1024)S(1)} %get-tuple-element.2849) | copy-start | bytes 24580
  113.0 3.7 collective-permute-start
  162.5 77.1 %all-gather.17.cloned.1.call-start = ((), (), s32[]{:S(2)}) async-start(), calls=%async_computation.3 | async-start | bytes 4718592 | tf_op jit(solution)/shard_map/all_gather | solution.py:34
  164.6 277.5 %all-gather.19.cloned.1.call-start = ((), (), s32[]{:S(2)}) async-start(), calls=%async_computation.4 | async-start | bytes 2359296 | tf_op jit(solution)/shard_map/all_gather | solution.py:59
  183.3 271.7 %all-gather.21.cloned.1.call-start = ((), (), s32[]{:S(2)}) async-start(), calls=%async_computation.5 | async-start | bytes 4718592 | tf_op jit(solution)/shard_map/all_gather | solution.py:59
  418.3 649.8 %all-reduce.22.cloned.1.call-start = ((), (), s32[]{:S(2)}) async-start(), calls=%async_computation.6 | async-start | bytes 68157440
  431.1 8.4 copy-start.26
  431.1 8.3 copy-start.39
  455.2 16.9 %copy-start.42 = (pred[64,64]{1,0:T(8,128)(4,1)S(1)}, pred[64,64]{1,0:T(8,128)(4,1)}, u32[]{:S(2)}) copy-start(pred[64,64]{1,0:T(8,128)(4,1)} %get-tuple-element.3960) | copy-start | bytes 12292
  455.2 16.9 %copy-start.87 = (f32[2,2,64]{2,1,0:T(2,128)S(1)}, f32[2,2,64]{2,1,0:T(2,128)}, u32[]{:S(2)}) copy-start(f32[2,2,64]{2,1,0:T(2,128)} %get-tuple-element.3846) | copy-start | bytes 3076
  455.2 16.9 %copy-start.90 = (f32[2,2,64]{2,1,0:T(2,128)S(1)}, f32[2,2,64]{2,1,0:T(2,128)}, u32[]{:S(2)}) copy-start(f32[2,2,64]{2,1,0:T(2,128)} %get-tuple-element.3848) | copy-start | bytes 3076
  455.2 16.9 %copy-start.104 = (f32[2,2,64,1]{2,1,3,0:T(2,128)S(1)}, f32[2,2,64,1]{2,1,3,0:T(2,128)}, u32[]{:S(2)}) copy-start(f32[2,2,64,1]{2,1,3,0:T(2,128)} %get-tuple-element.3843) | copy-start | bytes 3076
  455.2 16.9 %copy-start.107 = (f32[2,2,64,1]{2,1,3,0:T(2,128)S(1)}, f32[2,2,64,1]{2,1,3,0:T(2,128)}, u32[]{:S(2)}) copy-start(f32[2,2,64,1]{2,1,3,0:T(2,128)} %get-tuple-element.3842) | copy-start | bytes 3076
  546.1 3.1 collective-permute-start.1
  575.5 540.5 %copy-start.91 = (f32[14852]{0:T(1024)S(1)}, f32[14852]{0:T(1024)}, u32[]{:S(2)}) copy-start(f32[14852]{0:T(1024)} %param.38) | copy-start | bytes 178228
  575.5 540.5 %copy-start.92 = (f32[14852]{0:T(1024)S(1)}, f32[14852]{0:T(1024)}, u32[]{:S(2)}) copy-start(f32[14852]{0:T(1024)} %param.39) | copy-start | bytes 178228
  575.7 541.0 %copy-start.50 = (f32[131072]{0:T(1024)S(1)}, f32[131072]{0:T(1024)}, u32[]{:S(2)}) copy-start(f32[131072]{0:T(1024)} %param.31) | copy-start | bytes 1572868
  1069.9 49.4 %copy-start.44 = (f32[131072]{0:T(1024)}, f32[131072]{0:T(1024)S(1)}, u32[]{:S(2)}) copy-start(f32[131072]{0:T(1024)S(1)} %get-tuple-element.2774) | copy-start | bytes 1572868
  1071.9 47.4 %copy-start.41 = (f32[135168]{0:T(1024)}, f32[135168]{0:T(1024)S(1)}, u32[]{:S(2)}) copy-start(f32[135168]{0:T(1024)S(1)} %get-tuple-element.2772) | copy-start | bytes 1622020
  (151 other events, 465.9 us)
Sparse Core Ops, SparseCore 0:
  11.4 79.7 all-gather.10
  94.7 76.8 all-gather.12
  174.1 26.4 all-gather.14
  203.0 36.5 all-gather.16
  241.3 27.8 all-gather.18
  418.4 36.6 all-gather.20
  565.2 502.9 all-reduce.21
where the time goes:
time: 1140 us; the launch traced here: 1130 us
  waiting for transfers between devices  615 us (54%)
  other arithmetic  166 us (15%)
  matrix products  152 us (13%)
  local copies, waits for them, and re-layouts  120 us (11%)
  blocking collectives  40.8 us (4%)
  between operations  18.7 us (2%)
  loops' own time  12 us (1%)
    unnamed x8, waiting for transfers between devices  492 us
    another operation x34, other arithmetic, group_parts(): jax.scipy.linalg.solve_triangular(system, right_side, lower=True, unit_di...  86.5 us
    all_gather x1, waiting for transfers between devices, body(): lax.all_gather(mix_part, ('dp', 'ctx'), axis=0, tiled=True)  77.5 us
    psum x1, blocking collectives, body(): lax.psum((small_local, shard_squares), ('dp', 'ctx'))  40.8 us
    dot_general x17, matrix products, combine(): jnp.einsum('hij,hjk->hik', second_map, first_shift, precision=HIGHEST)  32.5 us
    all_gather x2, waiting for transfers between devices, entering(): lax.all_gather(part.astype(kind), axis)  31.5 us
  transfers between devices with their start and end apart: 9, of which 5 were waited for; matrix products, arithmetic and copies ran while one was open for 28% of the time, Pallas kernels for 0%

commit v1 on v0

--- a/solution.py
+++ b/solution.py
@@ -20,6 +20,18 @@
 CORRECT_TWO = 1.0 - 0.999**3
 MAX_NORM = 1.0
 HIGHEST = lax.Precision.HIGHEST
+
+
+def gather_by_bits(array, axis, dim):
+    ways, here, lap = (lax.axis_size(axis), lax.axis_index(axis), array.shape[dim])
+    line, have = (array, 1)
+    while have < ways:
+        line = jnp.concatenate(
+            [line, lax.ppermute(line, axis, [(d, (d - have) % ways) for d in range(ways)])],
+            axis=dim,
+        )
+        have = 2 * have
+    return jnp.roll(line, here * lap, axis=dim)
 
 
 def from_behind(value, axis, steps):
@@ -266,7 +278,7 @@
     mix_part = mixer_params.astype(jnp.bfloat16)
     ffn_part = ffn_params.astype(jnp.bfloat16)
     mix_whole, ffn_whole = (
-        lax.all_gather(mix_part, ("dp", "ctx"), axis=0, tiled=True),
+        gather_by_bits(mix_part, ("dp", "ctx"), 0),
         lax.all_gather(ffn_part, ("dp", "ctx"), axis=0, tiled=True),
     )
     w_in, w_out, w_ffn, w_down = split_weights(mix_whole, ffn_whole)

time: 1140 us -> 1380 us (1.21)
  waiting for transfers between devices: 615 us -> 804 us
  local copies, waits for them, and re-layouts: 120 us -> 159 us
    ppermute x0 -> x5, waiting for transfers between devices: none -> 258 us  [gather_by_bits(): lax.ppermute(line, axis, [(d, (d - have) % ways) for d in range(ways)])]
    all_gather x1 -> x0, waiting for transfers between devices: 77.5 us -> none  [body(): lax.all_gather(mix_part, ('dp', 'ctx'), axis=0, tiled=True)]
    unnamed x198 -> x196, local copies, waits for them, and re-layouts: 21.3 us -> 36.5 us
    all_gather x2, waiting for transfers between devices: 31.5 us -> 46.1 us  [entering(): lax.all_gather(part.astype(kind), axis)]
    unnamed x8 -> x7, waiting for transfers between devices: 492 us -> 487 us
  transfers between devices with their start and end apart: 9 -> 13, of which waited for: 5 -> 10; matrix products, arithmetic and copies ran while one was open for 28% -> 20% of each run, Pallas kernels for 0% -> 0%
where the time goes in v1:
time: 1380 us; the launch traced here: 1370 us
  waiting for transfers between devices  804 us (58%)
  other arithmetic  172 us (12%)
  local copies, waits for them, and re-layouts  159 us (12%)
  matrix products  156 us (11%)
  blocking collectives  40.8 us (3%)
  between operations  18.5 us (1%)
  starting transfers between devices  15.3 us (1%)
    unnamed x7, waiting for transfers between devices  487 us
    ppermute x5, waiting for transfers between devices, gather_by_bits(): lax.ppermute(line, axis, [(d, (d - have) % ways) for d in range(ways)])  258 us
    another operation x34, other arithmetic, group_parts(): jax.scipy.linalg.solve_triangular(system, right_side, lower=True, unit_di...  86.5 us
    all_gather x2, waiting for transfers between devices, entering(): lax.all_gather(part.astype(kind), axis)  46.1 us
    psum x1, blocking collectives, body(): lax.psum((small_local, shard_squares), ('dp', 'ctx'))  40.8 us
    unnamed x196, local copies, waits for them, and re-layouts  36.5 us
    dot_general x17, matrix products, combine(): jnp.einsum('hij,hjk->hik', second_map, first_shift, precision=HIGHEST)  32.6 us
  transfers between devices with their start and end apart: 13, of which 10 were waited for; matrix products, arithmetic and copies ran while one was open for 20% of the time, Pallas kernels for 0%

profile of v1, /device:TPU:0, one launch (start us, length us, event | category | flops | bytes accessed | tf_op | source)
XLA Modules:
  0.0 1366.6 jit_solution(3357960069091709359)
XLA Ops:
  9.0 6.4 collective-permute-start
  20.8 9.9 collective-permute-done.1
  32.6 23.5 %collective-permute-done.2 = bf16[524288]{0:T(1024)(128)(2,1)S(1)} collective-permute-done((bf16[524288]{0:T(1024)(128)(2,1)S(1)}, bf16[524288]{0:T(1024)(128)(2,1)S(1)}, u32[]{:S(2)}, u32[]{:S(2)}) %collective-permute-start.2) | collective-permute-done | bytes 1048608 | tf_op jit(solution)/shard_map/ppermute | solution.py:30
  60.9 43.5 %collective-permute-done.3 = bf16[1048576]{0:T(1024)(128)(2,1)S(1)} collective-permute-done((bf16[1048576]{0:T(1024)(128)(2,1)S(1)}, bf16[1048576]{0:T(1024)(128)(2,1)S(1)}, u32[]{:S(2)}, u32[]{:S(2)}) %collective-permute-start.3) | collective-permute-done | bytes 2097184 | tf_op jit(solution)/shard_map/ppermute | solution.py:30
  113.0 177.4 %collective-permute-done.4 = bf16[2097152]{0:T(1024)(128)(2,1)} collective-permute-done((bf16[2097152]{0:T(1024)(128)(2,1)}, bf16[2097152]{0:T(1024)(128)(2,1)}, u32[]{:S(2)}, u32[]{:S(2)}) %collective-permute-start.4) | collective-permute-done | bytes 4194336 | tf_op jit(solution)/shard_map/ppermute | solution.py:30
  302.8 6.4 dynamic-slice.10
  309.3 10.3 slice.251
  333.6 38.6 %while.160 = (s32[]{:T(128)}, f32[2,256,256]{2,1,0:T(8,128)}, f32[2,256,512]{2,1,0:T(8,128)}, f32[2,2,64]{2,1,0:T(2,128)}, f32[2,2,64,256]{3,2,1,0:T(8,128)S(1)}...) while((s32[]{:T(128)}, f32[2,256,256]{2,1,0:T(8,128)}, ...), condition=%wide.region_4.6_spmd.clone, body=%wide.region_2.5_spmd.clone.sunk | while | flops 1611903232 | bytes 17252060 | solution.py:241
  336.1 9.8 custom-call.57
  355.4 9.8 custom-call.57
  397.2 7.0 all-gather.12.cloned.1.call-done
  404.2 39.1 %all-gather.14.cloned.1.call-done = bf16[16,256,512]{2,1,0:T(8,128)(2,1)} async-done(((bf16[2,256,512]{2,1,0:T(8,128)(2,1)}), bf16[16,256,512]{2,1,0:T(8,128)(2,1)}) %all-gather.14.cloned.1.call-update) | async-done | bytes 4194320 | tf_op jit(solution)/shard_map/all_gather | solution.py:46
  443.3 16.6 %while.161 = (s32[]{:T(128)}, f32[2,256,512]{2,1,0:T(8,128)S(1)}, s32[]{:T(128)}, bf16[8,2,256,256]{3,2,1,0:T(8,128)(2,1)}, bf16[8,2,256,512]{3,2,1,0:T(8,128)(2,1)}, /*index=5*/s32[]{:T(128)}, s32[]{:T(128)}) while((s32[]{:T(128)}, f32[2,256,512]{2,1,0:T(8,128)S(1)}, s32[]{:T(128)}, bf16[8,2,256,256]{3,2,1,0:T(8,128)(2,1)}, ...), condition=%wide.region_6.8_spmd.clone, body=%wide.region_5.7_spmd.clone.sunk | while | flops 806617088 | bytes 6031975 | solution.py:63
  460.9 54.5 %while.156 = (s32[]{:T(128)}, f32[2,256,512]{2,1,0:T(8,128)S(1)}, f32[2,2,64,512]{3,2,1,0:T(8,128)}, f32[2,2,64]{2,1,0:T(2,128)}, f32[2,2,64,256]{3,2,1,0:T(8,12...) while((s32[]{:T(128)}, f32[2,256,512]{2,1,0:T(8,128)S(1)}, ...), condition=%wide.region_10.12_spmd, body=%wide.region_8.11_spmd.sunk | while | flops 781201600 | bytes 15006109 | solution.py:210
  470.4 11.2 custom-call.54
  497.7 11.2 custom-call.54
  526.6 65.1 %while.158 = (s32[]{:T(128)}, f32[2,256,512]{2,1,0:T(8,128)S(1)}, f32[2,2,64,64]{3,2,1,0:T(8,128)}, f32[2,2,64,64]{3,2,1,0:T(8,128)}, f32[2,2,64,1]{2,1,3,0:T(2,...) while((s32[]{:T(128)}, f32[2,256,512]{2,1,0:T(8,128)S(1)}, ...), condition=%wide.region_17.19_spmd.clone.clone, body=%wide.region_15.18_spmd.clone.clone.sunk | while | flops 529560128 | bytes 10851429 | solution.py:210
  535.5 11.2 custom-call.55
  568.1 11.2 custom-call.55
  591.7 6.1 slice.304
  597.8 9.7 slice.270
  610.6 15.2 %slice.274 = bf16[1408,1024]{1,0:T(8,128)(2,1)} reshape(bf16[1441792]{0:T(1024)(128)(2,1)} %slice.307) | data formatting | bytes 5767168 | tf_op jit(solution)/shard_map/slice | solution.py:122
  637.7 15.0 %while.162 = (s32[]{:T(128)}, f32[2,256,512]{2,1,0:T(8,128)S(1)}, f32[2,2,1,1]{1,3,2,0:T(1,128)}, f32[2,2,64,256]{3,2,1,0:T(8,128)}, f32[2,2,64,512]{3,2,1,0:T(8...) while((s32[]{:T(128)}, f32[2,256,512]{2,1,0:T(8,128)S(1)}, ...), condition=%wide.region_19.21_spmd.clone, body=%wide.region_18.20_spmd.clone.sunk | while | flops 655753216 | bytes 7277727 | solution.py:210
  667.4 8.3 copy.331
  678.5 12.1 all-gather.18.cloned.1.call-done
  690.7 13.4 while.157
  707.6 67.0 %while.159 = (s32[]{:T(128)}, f32[2,256,512]{2,1,0:T(8,128)S(1)}, f32[2,2,64,256]{3,2,0,1:T(8,128)}, f32[2,2,64,256]{3,2,0,1:T(8,128)}, f32[2,2,64,512]{3,2,0,1:...) while((s32[]{:T(128)}, f32[2,256,512]{2,1,0:T(8,128)S(1)}, ...), condition=%wide.region_33.35_spmd.clone.clone, body=%wide.region_22.34_spmd.clone.clone.sunk | while | flops 1569133696 | bytes 51536812 | solution.py:210
  714.4 9.8 custom-call.56
  747.7 9.8 custom-call.56
  794.6 8.1 copy.330
  819.1 486.7 %all-reduce.22.cloned.1.call-done = (f32[4194304]{0:T(1024)}, f32[4325376]{0:T(1024)}) async-done(((f32[4194304]{0:T(1024)}, f32[4325376]{0:T(1024)}), (f32[4194304]{0:T(1024)}, f32[4325376]{0:T(1024)})) %all-reduce.22.cloned.1.call-update) | async-done | bytes 34078736
  1310.9 40.8 %all-reduce.18 = (f32[14852]{0:T(1024)S(1)}, f32[]{:T(128)}) all-reduce(f32[14852]{0:T(1024)S(1)} %concatenate.67, f32[]{:T(128)S(6)} %add.463), channel_id=1, replica_groups=mesh['dp'=4,'ctx'=8] {'dp','ctx'}, use_global_device_ids=true, to_apply=%region_48.50 | all-reduce | flops 14853 | bytes 118824 | tf_op jit(solution)/shard_map/psum | solution.py:362
  (705 shorter events, 351.4 us)
Async XLA Ops:
  7.2 397.0 %all-gather.12.cloned.1.call-start = ((), (), s32[]{:S(2)}) async-start(), calls=%async_computation.1 | async-start | bytes 2359296 | tf_op jit(solution)/shard_map/all_gather | solution.py:46
  9.0 10.3 collective-permute-start
  19.3 11.3 collective-permute-start.1
  30.8 25.4 %collective-permute-start.2 = (bf16[524288]{0:T(1024)(128)(2,1)S(1)}, bf16[524288]{0:T(1024)(128)(2,1)S(1)}, u32[]{:S(2)}, u32[]{:S(2)}) collective-permute-start(bf16[524288]{0:T(1024)(128)(2,1)S(1)} %pad_maximum_fusion.2), channel_id=1, source_target_pairs={{0,28},{1,29},{2,30},{3,31},{4,0},{5,1},{6,2},{7,3},{8,4},{9,5},{1... | collective-permute-start | bytes 3145736 | tf_op jit(solution)/shard_map/ppermute | solution.py:30
  56.3 48.1 %collective-permute-start.3 = (bf16[1048576]{0:T(1024)(128)(2,1)S(1)}, bf16[1048576]{0:T(1024)(128)(2,1)S(1)}, u32[]{:S(2)}, u32[]{:S(2)}) collective-permute-start(bf16[1048576]{0:T(1024)(128)(2,1)S(1)} %pad_maximum_fusion), channel_id=1, source_target_pairs={{0,24},{1,25},{2,26},{3,27},{4,28},{5,29},{6,30},{7,31},{8,0},{9,1... | collective-permute-start | bytes 6291464 | tf_op jit(solution)/shard_map/ppermute | solution.py:30
  59.4 49.2 %copy-start.65 = (f32[14852]{0:T(1024)S(1)}, f32[14852]{0:T(1024)}, u32[]{:S(2)}) copy-start(f32[14852]{0:T(1024)} %param.37) | copy-start | bytes 178228
  60.9 48.3 %copy-start.11 = (bf16[1,128,1024]{2,1,0:T(8,128)(2,1)S(1)}, bf16[1,128,1024]{2,1,0:T(8,128)(2,1)}, u32[]{:S(2)}) copy-start(bf16[1,128,1024]{2,1,0:T(8,128)(2,1)} %param.29) | copy-start | bytes 786436
  108.2 182.3 %collective-permute-start.4 = (bf16[2097152]{0:T(1024)(128)(2,1)}, bf16[2097152]{0:T(1024)(128)(2,1)}, u32[]{:S(2)}, u32[]{:S(2)}) collective-permute-start(bf16[2097152]{0:T(1024)(128)(2,1)} %get-tuple-element.2837), channel_id=1, source_target_pairs={{0,16},{1,17},{2,18},{3,19},{4,20},{5,21},{6,22},{7,23},{8,24},{9,... | collective-permute-start | bytes 12582920 | tf_op jit(solution)/shard_map/ppermute | solution.py:30
  109.2 185.0 %copy-start.29 = (f32[1024,4]{1,0:T(8,128)}, f32[1024,4]{1,0:T(8,128)S(1)}, u32[]{:S(2)}) copy-start(f32[1024,4]{1,0:T(8,128)S(1)} %reshape.844) | copy-start | bytes 49156
  109.9 209.7 %copy-start.86 = (f32[128]{0:T(128)}, f32[128]{0:T(128)S(1)}, u32[]{:S(2)}) copy-start(f32[128]{0:T(128)S(1)} %fusion.309) | copy-start | bytes 1540
  110.6 209.0 %copy-start.68 = (f32[1024]{0:T(1024)}, f32[1024]{0:T(1024)S(1)}, u32[]{:S(2)}) copy-start(f32[1024]{0:T(1024)S(1)} %get-tuple-element.2854) | copy-start | bytes 12292
  113.0 214.4 %copy-start.75 = (f32[2048]{0:T(1024)}, f32[2048]{0:T(1024)S(1)}, u32[]{:S(2)}) copy-start(f32[2048]{0:T(1024)S(1)} %get-tuple-element.2855) | copy-start | bytes 24580
  113.0 214.4 %copy-start.77 = (f32[2048]{0:T(1024)}, f32[2048]{0:T(1024)S(1)}, u32[]{:S(2)}) copy-start(f32[2048]{0:T(1024)S(1)} %get-tuple-element.2856) | copy-start | bytes 24580
  113.0 214.4 %copy-start.79 = (f32[2048]{0:T(1024)}, f32[2048]{0:T(1024)S(1)}, u32[]{:S(2)}) copy-start(f32[2048]{0:T(1024)S(1)} %get-tuple-element.2857) | copy-start | bytes 24580
  113.0 214.4 %copy-start.81 = (f32[2048]{0:T(1024)}, f32[2048]{0:T(1024)S(1)}, u32[]{:S(2)}) copy-start(f32[2048]{0:T(1024)S(1)} %get-tuple-element.2858) | copy-start | bytes 24580
  324.6 2.8 collective-permute-start.5
  374.2 69.1 %all-gather.14.cloned.1.call-start = ((), (), s32[]{:S(2)}) async-start(), calls=%async_computation.2 | async-start | bytes 4718592 | tf_op jit(solution)/shard_map/all_gather | solution.py:46
  376.4 215.3 %all-gather.10.cloned.1.call-start = ((), (), s32[]{:S(2)}) async-start(), calls=%async_computation | async-start | bytes 8921088 | tf_op jit(solution)/shard_map/all_gather | solution.py:282
  378.5 300.0 %all-gather.16.cloned.1.call-start = ((), (), s32[]{:S(2)}) async-start(), calls=%async_computation.3 | async-start | bytes 2359296 | tf_op jit(solution)/shard_map/all_gather | solution.py:71
  397.1 293.4 %all-gather.18.cloned.1.call-start = ((), (), s32[]{:S(2)}) async-start(), calls=%async_computation.4 | async-start | bytes 4718592 | tf_op jit(solution)/shard_map/all_gather | solution.py:71
  653.5 652.3 %all-reduce.22.cloned.1.call-start = ((), (), s32[]{:S(2)}) async-start(), calls=%async_computation.5 | async-start | bytes 68157440
  690.7 16.9 %copy-start.43 = (pred[64,64]{1,0:T(8,128)(4,1)S(1)}, pred[64,64]{1,0:T(8,128)(4,1)}, u32[]{:S(2)}) copy-start(pred[64,64]{1,0:T(8,128)(4,1)} %get-tuple-element.3973) | copy-start | bytes 12292
  690.7 16.9 %copy-start.83 = (f32[2,2,64]{2,1,0:T(2,128)S(1)}, f32[2,2,64]{2,1,0:T(2,128)}, u32[]{:S(2)}) copy-start(f32[2,2,64]{2,1,0:T(2,128)} %get-tuple-element.3856) | copy-start | bytes 3076
  690.7 16.9 %copy-start.84 = (f32[2,2,64]{2,1,0:T(2,128)S(1)}, f32[2,2,64]{2,1,0:T(2,128)}, u32[]{:S(2)}) copy-start(f32[2,2,64]{2,1,0:T(2,128)} %get-tuple-element.3858) | copy-start | bytes 3076
  690.7 16.9 %copy-start.91 = (f32[2,2,64,1]{2,1,3,0:T(2,128)S(1)}, f32[2,2,64,1]{2,1,3,0:T(2,128)}, u32[]{:S(2)}) copy-start(f32[2,2,64,1]{2,1,3,0:T(2,128)} %get-tuple-element.3853) | copy-start | bytes 3076
  783.5 3.2 collective-permute-start.6
  815.9 539.3 %copy-start.50 = (f32[131072]{0:T(1024)S(1)}, f32[131072]{0:T(1024)}, u32[]{:S(2)}) copy-start(f32[131072]{0:T(1024)} %param.31) | copy-start | bytes 1572868
  815.9 541.9 %copy-start.41 = (f32[135168]{0:T(1024)S(1)}, f32[135168]{0:T(1024)}, u32[]{:S(2)}) copy-start(f32[135168]{0:T(1024)} %param.34) | copy-start | bytes 1622020
  815.9 541.9 %copy-start.60 = (f32[135168]{0:T(1024)S(1)}, f32[135168]{0:T(1024)}, u32[]{:S(2)}) copy-start(f32[135168]{0:T(1024)} %param.35) | copy-start | bytes 1622020
  815.9 541.9 %copy-start.61 = (f32[135168]{0:T(1024)S(1)}, f32[135168]{0:T(1024)}, u32[]{:S(2)}) copy-start(f32[135168]{0:T(1024)} %param.36) | copy-start | bytes 1622020
  1307.6 51.7 %copy-start.45 = (f32[131072]{0:T(1024)}, f32[131072]{0:T(1024)S(1)}, u32[]{:S(2)}) copy-start(f32[131072]{0:T(1024)S(1)} %get-tuple-element.2774) | copy-start | bytes 1572868
  1309.6 49.7 %copy-start.42 = (f32[135168]{0:T(1024)}, f32[135168]{0:T(1024)S(1)}, u32[]{:S(2)}) copy-start(f32[135168]{0:T(1024)S(1)} %get-tuple-element.2772) | copy-start | bytes 1622020
  (123 other events, 612.7 us)
Sparse Core Ops, SparseCore 0:
  374.3 29.8 all-gather.11
  406.7 36.5 all-gather.13
  446.8 78.5 all-gather.9
  527.1 26.7 all-gather.15
  653.6 36.8 all-gather.17
  802.8 502.9 all-reduce.21
